TPU v7x, 256 devices: a whole 4x4x8 slice. The times are simulated.
256 devices in a mesh: gx: 32 (over z, x), gy: 8 (over y, core).
Axes of the slice: x: 4, y: 4, z: 8, core: 2. Of those that a mesh axis runs over, the one named last changes fastest.
Arguments:
- field: bfloat16 [20, 256, 128, 256], P(None, 'gx', 'gy'), may hold values from -6 to 6
- cotangent: bfloat16 [20, 256, 128, 256], P(None, 'gx', 'gy'), may hold values from -6 to 6
- spectral_weight: bfloat16 [2, 20, 20, 24, 2304], P(None, None, None, 'gy', 'gx'), may hold values from -6 to 6
- pointwise_weight: bfloat16 [20, 20], replicated, may hold values from -1.25 to 1.25
- bias: float32 [20], replicated, may hold values from -1 to 1
Outputs:
- output: bfloat16 [20, 256, 128, 256], P(None, 'gx', 'gy')
- grad_field: bfloat16 [20, 256, 128, 256], P(None, 'gx', 'gy')
- grad_spectral: float32 [2, 20, 20, 24, 2304], P(None, None, None, 'gy', 'gx')
- grad_pointwise: float32 [20, 20], replicated
- grad_bias: float32 [20], replicated
All inputs are finite; a program needn't handle non-finite values.
Results may differ from a plain program's by a relative error of at most 0.0013.
Values sent between devices are 32-bit elements; how exact they have to be, the bound alone decides.
A program may use at most 128 MiB of HBM per device.

v0:
```python
import math
import jax
import jax.numpy as jnp
from jax import lax
from jax.sharding import PartitionSpec as P

MX = 24
MY = 24
MZ = 24
PRECISE = lax.Precision.HIGHEST
TWO_PI = 2.0 * math.pi


def angles(frequencies, places, length):
    product = places[:, None] * frequencies[None, :] % length
    return product.astype(jnp.float32) * (TWO_PI / length)


def frequency(position, kept_modes, length):
    return jnp.where(position < kept_modes, position, position - 2 * kept_modes + length)


def forward_y(values, phases):
    cosine_table = jnp.cos(phases)
    sine_table = jnp.sin(phases)
    with_cos = jnp.einsum("brcxy,yj->brcxj", values, cosine_table, precision=PRECISE)
    with_sin = jnp.einsum("brcxy,yj->brcxj", values, sine_table, precision=PRECISE)
    real_part = with_cos[:, 0] + with_sin[:, 1]
    imag_part = with_cos[:, 1] - with_sin[:, 0]
    return jnp.stack([real_part, imag_part], axis=1)


def inverse_y(values, phases):
    cosine_table = jnp.cos(phases)
    sine_table = jnp.sin(phases)
    with_cos = jnp.einsum("brcxj,yj->brcxy", values, cosine_table, precision=PRECISE)
    with_sin = jnp.einsum("brcxj,yj->brcxy", values, sine_table, precision=PRECISE)
    real_part = with_cos[:, 0] - with_sin[:, 1]
    imag_part = with_sin[:, 0] + with_cos[:, 1]
    return jnp.stack([real_part, imag_part], axis=1)


def local(field, cotangent, spectral_weight, pointwise_weight, bias):
    channels, rows_x, rows_y, depth_cells = field.shape
    blocks_z = spectral_weight.shape[3]
    pair_rows = spectral_weight.shape[4]
    width_x = 2 * MX
    width_y = 2 * MY
    full_x = rows_x * lax.axis_size("gx")
    full_y = rows_y * lax.axis_size("gy")
    cell_count = float(full_x * full_y * depth_cells)
    place_x = lax.axis_index("gx")
    place_y = lax.axis_index("gy")
    own_x = place_x * rows_x + jnp.arange(rows_x, dtype=jnp.int32)
    freq_x = frequency(jnp.arange(width_x, dtype=jnp.int32), MX, full_x)
    freq_y = frequency(jnp.arange(width_y, dtype=jnp.int32), MY, full_y)
    phases_full_y = angles(freq_y, jnp.arange(full_y, dtype=jnp.int32), full_y)
    z_phases = angles(
        jnp.arange(MZ, dtype=jnp.int32), jnp.arange(depth_cells, dtype=jnp.int32), depth_cells
    )
    table_z = jnp.stack([jnp.cos(z_phases), -jnp.sin(z_phases)], axis=2).reshape(
        depth_cells, 2 * MZ
    )
    kz_own = place_y * blocks_z + jnp.arange(blocks_z, dtype=jnp.int32)
    weight_z = (jnp.where(kz_own == 0, 1.0, 2.0).astype(jnp.float32) / cell_count)[None, :, None]
    own_first = place_x * pair_rows
    flat_width = blocks_z * 2 * channels

    def kx_terms(values, places, first_pair, count):
        kx_count = min(count // width_y + 2, width_x)
        kx_first = jnp.minimum(first_pair // width_y, width_x - kx_count)
        kx_ids = kx_first + jnp.arange(kx_count, dtype=jnp.int32)
        phases = angles(frequency(kx_ids, MX, full_x), places, full_x)
        cosine_table = jnp.cos(phases)
        sine_table = jnp.sin(phases)
        real_part = jnp.einsum(
            "bcxj,xi->ijbc", values[:, 0], cosine_table, precision=PRECISE
        ) + jnp.einsum("bcxj,xi->ijbc", values[:, 1], sine_table, precision=PRECISE)
        imag_part = jnp.einsum(
            "bcxj,xi->ijbc", values[:, 1], cosine_table, precision=PRECISE
        ) - jnp.einsum("bcxj,xi->ijbc", values[:, 0], sine_table, precision=PRECISE)
        terms = jnp.stack([real_part, imag_part], axis=3).reshape(kx_count * width_y, flat_width)
        offset = first_pair - kx_first * width_y
        return lax.dynamic_slice_in_dim(terms, offset, count, 0)

    def analyze(values):
        flat = values.reshape(-1, depth_cells)
        spectra = jnp.einsum("zk,mz->km", table_z, flat, precision=PRECISE).reshape(
            2 * MZ, channels, rows_x, rows_y
        )
        columns = lax.all_to_all(spectra, "gy", split_axis=0, concat_axis=3, tiled=True)
        mode_data = forward_y(columns.reshape(blocks_z, 2, channels, rows_x, full_y), phases_full_y)
        portion = lax.all_gather(mode_data, "gx", axis=3, tiled=True)
        places = jnp.arange(portion.shape[3], dtype=jnp.int32)
        owned = kx_terms(portion, places, own_first, pair_rows)
        return jnp.transpose(owned.reshape(pair_rows, blocks_z, 2, channels), (2, 3, 1, 0))

    def synthesize(spectrum):
        portion = lax.all_gather(spectrum, "gx", axis=3, tiled=True)
        blocks = portion.reshape(2, channels, blocks_z, width_x, width_y)
        phases = angles(freq_x, own_x, full_x)
        cosine_table = jnp.cos(phases)
        sine_table = jnp.sin(phases)
        real_part = jnp.einsum(
            "cbij,xi->bcxj", blocks[0], cosine_table, precision=PRECISE
        ) - jnp.einsum("cbij,xi->bcxj", blocks[1], sine_table, precision=PRECISE)
        imag_part = jnp.einsum(
            "cbij,xi->bcxj", blocks[0], sine_table, precision=PRECISE
        ) + jnp.einsum("cbij,xi->bcxj", blocks[1], cosine_table, precision=PRECISE)
        mode_data = jnp.stack([real_part, imag_part], axis=1)
        fields = inverse_y(mode_data, phases_full_y)
        columns = lax.all_to_all(fields, "gy", split_axis=4, concat_axis=0, tiled=True)
        flat = columns.reshape(2 * MZ, -1)
        return jnp.einsum("km,zk->mz", flat, table_z, precision=PRECISE).reshape(
            channels, rows_x, rows_y, depth_cells
        )

    weights = spectral_weight.astype(jnp.float32)
    widened = field.astype(jnp.float32)
    spec_u = analyze(widened)
    mixed_re = jnp.einsum("cobp,cbp->obp", weights[0], spec_u[0], precision=PRECISE) - jnp.einsum(
        "cobp,cbp->obp", weights[1], spec_u[1], precision=PRECISE
    )
    mixed_im = jnp.einsum("cobp,cbp->obp", weights[0], spec_u[1], precision=PRECISE) + jnp.einsum(
        "cobp,cbp->obp", weights[1], spec_u[0], precision=PRECISE
    )
    mixed_modes = jnp.stack([mixed_re, mixed_im]) * weight_z
    conv = synthesize(mixed_modes)
    pointwise = jnp.dot(
        pointwise_weight.T, field.reshape(channels, -1), preferred_element_type=jnp.float32
    ).reshape(field.shape)
    preact = pointwise + bias[:, None, None, None] + conv
    activated, pullback = jax.vjp(jax.nn.gelu, preact)
    gradient = pullback(cotangent.astype(jnp.float32))[0]
    grad_mix = analyze(gradient) * weight_z
    spec_re = jnp.einsum("cobp,obp->cbp", weights[0], grad_mix[0], precision=PRECISE) + jnp.einsum(
        "cobp,obp->cbp", weights[1], grad_mix[1], precision=PRECISE
    )
    spec_im = jnp.einsum("cobp,obp->cbp", weights[0], grad_mix[1], precision=PRECISE) - jnp.einsum(
        "cobp,obp->cbp", weights[1], grad_mix[0], precision=PRECISE
    )
    grad_spec = jnp.stack([spec_re, spec_im])
    weight_re = jnp.einsum("cbp,obp->cobp", spec_u[0], grad_mix[0], precision=PRECISE) + jnp.einsum(
        "cbp,obp->cobp", spec_u[1], grad_mix[1], precision=PRECISE
    )
    weight_im = jnp.einsum("cbp,obp->cobp", spec_u[0], grad_mix[1], precision=PRECISE) - jnp.einsum(
        "cbp,obp->cobp", spec_u[1], grad_mix[0], precision=PRECISE
    )
    grad_spectral = jnp.stack([weight_re, weight_im])
    returned = synthesize(grad_spec)
    grad_flat = gradient.reshape(channels, -1)
    back_point = jnp.dot(
        pointwise_weight.astype(jnp.float32), grad_flat, precision=PRECISE
    ).reshape(field.shape)
    grad_field = (back_point + returned).astype(jnp.bfloat16)
    local_weight = jnp.dot(widened.reshape(channels, -1), grad_flat.T, precision=PRECISE)
    local_bias = jnp.sum(grad_flat, axis=1)
    summed_weight, summed_bias = lax.psum((local_weight, local_bias), ("gx", "gy"))
    shrink = cell_count ** (-0.5)
    return (
        activated.astype(jnp.bfloat16),
        grad_field,
        grad_spectral,
        summed_weight * shrink,
        summed_bias * shrink,
    )


def solution(mesh):
    placed = (
        P(None, "gx", "gy", None),
        P(None, "gx", "gy", None),
        P(None, None, None, "gy", "gx"),
        P(),
        P(),
    )
    return jax.shard_map(
        local,
        mesh=mesh,
        in_specs=placed,
        out_specs=(
            P(None, "gx", "gy", None),
            P(None, "gx", "gy", None),
            P(None, None, None, "gy", "gx"),
            P(),
            P(),
        ),
        check_vma=False,
    )
```

profile of v0, /device:TPU:1, one launch (start us, length us, event | category | flops | bytes accessed | tf_op | source)
XLA Modules:
  0.0 803.7 jit_solution(9280649417124723916)
XLA Ops:
  14.2 5.5 reshape.223
  19.7 6.6 all-to-all-start
  26.5 9.0 %all-to-all-done = f32[8,1,15360]{2,1,0:T(1,128)S(1)} async-done(((f32[8,1,15360]{2,1,0:T(1,128)}), f32[8,1,15360]{2,1,0:T(1,128)S(1)}, u32[]{:S(2)}, u32[]{:S(2)}) %all-to-all-start) | async-done | bytes 491552 | tf_op jit(solution)/shard_map/all_to_all | solution.py:91
  37.9 5.3 reshape.224
  43.3 6.3 copy.295
  56.2 141.7 %all-gather.5.cloned.1.call-done = f32[3,2,20,256,48]{4,3,2,1,0:T(8,128)} async-done(((f32[3,2,20,8,48]{4,3,2,1,0:T(8,128)}), f32[3,2,20,256,48]{4,3,2,1,0:T(8,128)}) %all-gather.5.cloned.1.call-update) | async-done | bytes 5898256 | tf_op jit(solution)/shard_map/all_gather | solution.py:93
  197.9 7.2 fusion
  205.2 7.1 fusion.1
  222.3 91.0 %all-gather.7.cloned.1.call-done = f32[2,20,3,2304]{1,0,2,3:T(2,128)} async-done(((f32[2,20,3,72]{1,0,2,3:T(2,128)}), f32[2,20,3,2304]{1,0,2,3:T(2,128)}) %all-gather.7.cloned.1.call-update) | async-done | bytes 1105936 | tf_op jit(solution)/shard_map/all_gather | solution.py:99
  313.3 10.0 %fusion.244 = (f32[1,20,3,2304]{1,0,2,3:T(1,128)}, f32[1,20,3,2304]{1,0,2,3:T(1,128)}) fusion(f32[2,20,3,2304]{1,0,2,3:T(2,128)} %all-gather.7.cloned.1.call-done), kind=kLoop, calls=%fused_computation.296 | loop fusion | bytes 2211840 | tf_op jit(solution)/shard_map/slice | solution.py:106
  323.3 11.2 %copy.429 = f32[1,20,3,2304]{3,2,1,0:T(4,128)} copy(f32[1,20,3,2304]{1,0,2,3:T(1,128)} %get-tuple-element.59) | data formatting | bytes 1105920 | tf_op jit(solution)/shard_map/squeeze | solution.py:105
  339.8 11.2 %copy.430 = f32[1,20,3,2304]{3,2,1,0:T(4,128)} copy(f32[1,20,3,2304]{1,0,2,3:T(1,128)} %get-tuple-element.58) | data formatting | bytes 1105920 | tf_op jit(solution)/shard_map/squeeze | solution.py:106
  360.5 5.6 reshape.225
  366.0 5.4 all-to-all-start.1
  374.4 6.1 all-to-all-done.1
  382.4 5.4 reshape.226
  387.8 5.8 copy.314
  399.4 10.1 %fusion.241 = (f32[20]{0:T(128)}, f32[20,8,16,256]{3,0,2,1:T(8,128)S(1)}, bf16[20,8,16,256]{3,0,2,1:T(8,128)(2,1)}) fusion(bf16[20,8,16,256]{3,2,1,0:T(8,128)(2,1)} %param.6, f32[256,48,1,1]{0,1,2,3:T(8,128)S(1)} %reshape.194, f32[20,8,16,48]{3,2,1,0:T(8,128)} %bitcast.337, f32[20,8,16,256]{3,0,2,1:T(8,128)} %fusion.18, f32[20]{0:T(128)S(1)} %copy-done.25), kind=kOutput, calls=%fused_computation.294 | convolution fusion | flops 393871360 | bytes 8405152 | tf_op jit(solution)/shard_map/km,zk->mz/dot_general | solution.py:114
  417.5 5.3 reshape.227
  422.8 12.3 %all_to_all.60 = f32[8,1,15360]{2,1,0:T(1,128)S(1)} all-to-all(f32[8,1,15360]{2,1,0:T(1,128)S(1)} %reshape.227), channel_id=1, replica_groups=mesh['gx'=32,'gy'=8] {'gy'}, dimensions={0} | all-to-all | bytes 983040 | tf_op jit(solution)/shard_map/all_to_all | solution.py:91
  437.0 5.3 reshape.228
  442.3 6.3 copy.320
  454.3 137.9 %all-gather.9.cloned.1.call-done = f32[3,2,20,256,48]{4,3,2,1,0:T(8,128)} async-done(((f32[3,2,20,8,48]{4,3,2,1,0:T(8,128)}), f32[3,2,20,256,48]{4,3,2,1,0:T(8,128)}) %all-gather.9.cloned.1.call-update) | async-done | bytes 5898256 | tf_op jit(solution)/shard_map/all_gather | solution.py:93
  592.2 7.2 fusion.4
  599.4 7.1 fusion.5
  627.0 78.9 %all-reduce = (f32[20,20]{0,1:T(8,128)S(1)}, f32[20]{0:T(128)S(1)}) all-reduce(f32[20,20]{0,1:T(8,128)S(1)} %fusion.36, f32[20]{0:T(128)S(1)} %copy-done.24), channel_id=1, replica_groups=mesh['gx'=32,'gy'=8] {'gx','gy'}, use_global_device_ids=true, to_apply=%region_0.1 | all-reduce | flops 420 | bytes 3360 | tf_op jit(solution)/shard_map/psum | solution.py:158
  711.0 10.0 %fusion.243 = (f32[1,20,3,2304]{1,0,2,3:T(1,128)}, f32[1,20,3,2304]{1,0,2,3:T(1,128)}) fusion(f32[2,20,3,2304]{1,0,2,3:T(2,128)} %all-gather.11.cloned.1.call-done), kind=kLoop, calls=%fused_computation.295 | loop fusion | bytes 2211840 | tf_op jit(solution)/shard_map/slice | solution.py:106
  721.0 9.8 %copy.433 = f32[1,20,3,2304]{3,2,1,0:T(4,128)S(1)} copy(f32[1,20,3,2304]{1,0,2,3:T(1,128)} %get-tuple-element.57) | data formatting | bytes 1105920 | tf_op jit(solution)/shard_map/squeeze | solution.py:105
  735.0 9.8 %copy.434 = f32[1,20,3,2304]{3,2,1,0:T(4,128)S(1)} copy(f32[1,20,3,2304]{1,0,2,3:T(1,128)} %get-tuple-element.56) | data formatting | bytes 1105920 | tf_op jit(solution)/shard_map/squeeze | solution.py:106
  753.3 5.7 reshape.229
  776.0 5.3 reshape.230
  781.4 5.8 copy.337
  (162 shorter events, 131.5 us)
Async XLA Ops:
  8.5 401.0 %copy-start.10 = (f32[256,48,1,1]{0,1,2,3:T(8,128)}, f32[256,48,1,1]{0,1,2,3:T(8,128)S(1)}, u32[]{:S(2)}) copy-start(f32[256,48,1,1]{0,1,2,3:T(8,128)S(1)} %reshape.194) | copy-start | bytes 147460
  19.7 15.8 %all-to-all-start = ((f32[8,1,15360]{2,1,0:T(1,128)}), f32[8,1,15360]{2,1,0:T(1,128)S(1)}, u32[]{:S(2)}, u32[]{:S(2)}) async-start(f32[8,1,15360]{2,1,0:T(1,128)} %reshape.223), calls=%async_computation | async-start | bytes 983040 | tf_op jit(solution)/shard_map/all_to_all | solution.py:91
  26.4 171.6 %all-gather.5.cloned.1.call-start = ((), (), s32[]{:S(2)}) async-start(), calls=%async_computation.4 | async-start | bytes 16220160 | tf_op jit(solution)/shard_map/all_gather | solution.py:93
  52.7 2.7 copy-start.9
  55.0 258.3 %all-gather.7.cloned.1.call-start = ((), (), s32[]{:S(2)}) async-start(), calls=%async_computation.5 | async-start | bytes 7299072 | tf_op jit(solution)/shard_map/all_gather | solution.py:99
  55.3 161.3 %copy-start.18 = (s32[3]{0:T(128)}, s32[3]{0:T(128)S(1)}, u32[]{:S(2)}) copy-start(s32[3]{0:T(128)S(1)} %compare_select_fusion) | copy-start | bytes 40
  55.3 165.9 %copy-start.22 = (f32[3]{0:T(128)}, f32[3]{0:T(128)S(1)}, u32[]{:S(2)}) copy-start(f32[3]{0:T(128)S(1)} %fusion.144) | copy-start | bytes 40
  56.2 164.7 %copy-start.5 = (bf16[1,20,20,3,72]{4,0,3,2,1:T(2,128)(2,1)}, bf16[1,20,20,3,72]{4,0,3,2,1:T(2,128)(2,1)S(1)}, u32[]{:S(2)}) copy-start(bf16[1,20,20,3,72]{4,0,3,2,1:T(2,128)(2,1)S(1)} %get-tuple-element.70) | copy-start | bytes 518404
  197.9 14.3 %copy-start.1 = (f32[3,2,20,256,48]{4,3,2,1,0:T(8,128)S(1)}, f32[3,2,20,256,48]{4,3,2,1,0:T(8,128)}, u32[]{:S(2)}) copy-start(f32[3,2,20,256,48]{4,3,2,1,0:T(8,128)} %all-gather.5.cloned.1.call-done) | copy-start | bytes 17694724
  220.8 102.5 %copy-start.12 = (f32[3,72,20]{1,0,2:T(4,128)}, f32[3,72,20]{1,0,2:T(4,128)S(1)}, u32[]{:S(2)}) copy-start(f32[3,72,20]{1,0,2:T(4,128)S(1)} %copy.440) | copy-start | bytes 51844
  220.8 102.5 %copy-start.14 = (f32[3,72,20]{1,0,2:T(4,128)}, f32[3,72,20]{1,0,2:T(4,128)S(1)}, u32[]{:S(2)}) copy-start(f32[3,72,20]{1,0,2:T(4,128)S(1)} %copy.439) | copy-start | bytes 51844
  222.2 132.6 %copy-start.16 = (s32[8]{0:T(128)}, s32[8]{0:T(128)S(1)}, u32[]{:S(2)}) copy-start(s32[8]{0:T(128)S(1)} %iota_add_fusion.1) | copy-start | bytes 100
  360.5 11.1 %copy-start.20 = (bf16[20,20]{1,0:T(8,128)(2,1)S(1)}, bf16[20,20]{1,0:T(8,128)(2,1)}, u32[]{:S(2)}) copy-start(bf16[20,20]{1,0:T(8,128)(2,1)} %param.8) | copy-start | bytes 2404
  366.0 14.5 %all-to-all-start.1 = ((f32[8,1,15360]{2,1,0:T(1,128)}), f32[8,1,15360]{2,1,0:T(1,128)S(1)}, u32[]{:S(2)}, u32[]{:S(2)}) async-start(f32[8,1,15360]{2,1,0:T(1,128)} %reshape.225), calls=%async_computation.1 | async-start | bytes 983040 | tf_op jit(solution)/shard_map/all_to_all | solution.py:112
  371.4 220.8 %all-gather.9.cloned.1.call-start = ((), (), s32[]{:S(2)}) async-start(), calls=%async_computation.6 | async-start | bytes 16220160 | tf_op jit(solution)/shard_map/all_gather | solution.py:93
  393.6 5.8 copy-start.25
  409.5 1.6 copy-start.3
  451.7 140.5 %copy-start.19 = (s32[3]{0:T(128)S(1)}, s32[3]{0:T(128)}, u32[]{:S(2)}) copy-start(s32[3]{0:T(128)} %copy-done.18) | copy-start | bytes 40
  454.0 257.0 %all-gather.11.cloned.1.call-start = ((), (), s32[]{:S(2)}) async-start(), calls=%async_computation.7 | async-start | bytes 7299072 | tf_op jit(solution)/shard_map/all_gather | solution.py:99
  592.2 14.3 %copy-start.2 = (f32[3,2,20,256,48]{4,3,2,1,0:T(8,128)S(1)}, f32[3,2,20,256,48]{4,3,2,1,0:T(8,128)}, u32[]{:S(2)}) copy-start(f32[3,2,20,256,48]{4,3,2,1,0:T(8,128)} %all-gather.9.cloned.1.call-done) | copy-start | bytes 17694724
  610.3 4.5 copy-start.23
  610.3 4.6 copy-start.6
  610.3 4.6 copy-start.13
  610.4 4.6 copy-start.15
  620.8 3.6 copy-start.4
  624.4 2.7 copy-start.24
  624.4 81.6 %copy-start.21 = (bf16[20,20]{1,0:T(8,128)(2,1)S(1)}, bf16[20,20]{1,0:T(8,128)(2,1)}, u32[]{:S(2)}) copy-start(bf16[20,20]{1,0:T(8,128)(2,1)} %param.8) | copy-start | bytes 2404
  721.0 10.9 %copy-start.17 = (s32[8]{0:T(128)S(1)}, s32[8]{0:T(128)}, u32[]{:S(2)}) copy-start(s32[8]{0:T(128)} %copy-done.16) | copy-start | bytes 100
  759.0 15.2 %all-to-all-start.3 = ((f32[8,1,15360]{2,1,0:T(1,128)}), f32[8,1,15360]{2,1,0:T(1,128)S(1)}, u32[]{:S(2)}, u32[]{:S(2)}) async-start(f32[8,1,15360]{2,1,0:T(1,128)} %reshape.229), calls=%async_computation.3 | async-start | bytes 983040 | tf_op jit(solution)/shard_map/all_to_all | solution.py:112
  769.7 2.3 copy-start.7
  769.8 2.3 copy-start.8
  787.2 4.8 copy-start.11
  (1 other events, 1.3 us)
Sparse Core Ops, SparseCore 0:
  55.1 142.7 all-gather.4
  222.3 90.9 all-gather.6
  454.2 137.9 all-gather.8
  617.8 91.3 all-gather.10
where the time goes:
time: 811 us; the launch traced here: 804 us
  waiting for transfers between devices  386 us (48%)
  local copies, waits for them, and re-layouts  188 us (23%)
  matrix products  93.9 us (12%)
  blocking collectives  91.2 us (11%)
  starting transfers between devices  17.2 us (2%)
  between operations  14.7 us (2%)
  other arithmetic  12.6 us (2%)
    all_gather x2, waiting for transfers between devices, analyze(): portion = lax.all_gather(mode_data, 'gx', axis=3, tiled=True)  280 us
    all_gather x2, waiting for transfers between devices, synthesize(): portion = lax.all_gather(spectrum, 'gx', axis=3, tiled=True)  91 us
    psum x1, blocking collectives, local(): lax.psum((local_weight, local_bias), ('gx', 'gy'))  78.9 us
    unnamed x71, local copies, waits for them, and re-layouts  60.5 us
    squeeze x4, local copies, waits for them, and re-layouts, synthesize(): blocks[0]  24.1 us
    squeeze x4, local copies, waits for them, and re-layouts, synthesize(): blocks[1]  24.1 us
    slice x2, local copies, waits for them, and re-layouts, synthesize(): blocks[1]  20.1 us
  transfers between devices with their start and end apart: 7, of which 5 were waited for; matrix products, arithmetic and copies ran while one was open for 4% of the time, Pallas kernels for 0%

commit v1 on v0

--- a/solution.py
+++ b/solution.py
@@ -1,3 +1,4 @@
+import functools
 import math
 import jax
 import jax.numpy as jnp
@@ -9,6 +10,22 @@
 MZ = 24
 PRECISE = lax.Precision.HIGHEST
 TWO_PI = 2.0 * math.pi
+
+
+def check_ports(local_block, group_axis):
+    m_next = jnp.concatenate(
+        lax.all_to_all(
+            jnp.stack([local_block for _ in range(lax.axis_size(group_axis))]),
+            split_axis=0,
+            axis_name=group_axis,
+            concat_axis=0,
+        ),
+        axis=3,
+    )
+    return m_next
+
+
+keep_up_the_bench = functools.partial(check_ports, group_axis="gx")
 
 
 def angles(frequencies, places, length):
@@ -90,7 +107,7 @@
         )
         columns = lax.all_to_all(spectra, "gy", split_axis=0, concat_axis=3, tiled=True)
         mode_data = forward_y(columns.reshape(blocks_z, 2, channels, rows_x, full_y), phases_full_y)
-        portion = lax.all_gather(mode_data, "gx", axis=3, tiled=True)
+        portion = keep_up_the_bench(mode_data)
         places = jnp.arange(portion.shape[3], dtype=jnp.int32)
         owned = kx_terms(portion, places, own_first, pair_rows)
         return jnp.transpose(owned.reshape(pair_rows, blocks_z, 2, channels), (2, 3, 1, 0))

time: 811 us -> 1020 us (1.26)
  waiting for transfers between devices: 386 us -> 239 us
  blocking collectives: 91.2 us -> 226 us
  other arithmetic: 12.6 us -> 119 us
  local copies, waits for them, and re-layouts: 188 us -> 292 us
  starting transfers between devices: 17.2 us -> 27.7 us
    all_gather x2 -> x0, waiting for transfers between devices: 280 us -> none  [analyze(): portion = lax.all_gather(mode_data, 'gx', axis=3, tiled=True)]
    all_to_all x0 -> x1, blocking collectives: none -> 136 us  [check_ports(): lax.all_to_all(jnp.stack([local_block for _ in range(lax.axis_size(group_...]
    all_to_all x0 -> x1, waiting for transfers between devices: none -> 128 us  [check_ports(): lax.all_to_all(jnp.stack([local_block for _ in range(lax.axis_size(group_...]
    all_to_all x0 -> x2, other arithmetic: none -> 108 us  [check_ports(): lax.all_to_all(jnp.stack([local_block for _ in range(lax.axis_size(group_...]
    unnamed x71 -> x75, local copies, waits for them, and re-layouts: 60.5 us -> 123 us
    reshape x0 -> x2, local copies, waits for them, and re-layouts: none -> 26.4 us  [check_ports(): jnp.concatenate(lax.all_to_all(jnp.stack([local_block for _ in range(lax....]
    another operation x0 -> x2, local copies, waits for them, and re-layouts: none -> 14.9 us  [check_ports(): jnp.stack([local_block for _ in range(lax.axis_size(group_axis))])]
    all_to_all x0 -> x1, starting transfers between devices: none -> 10.6 us  [check_ports(): lax.all_to_all(jnp.stack([local_block for _ in range(lax.axis_size(group_...]
  transfers between devices with their start and end apart: 7 -> 6, of which waited for: 5 -> 4; matrix products, arithmetic and copies ran while one was open for 4% -> 3% of each run, Pallas kernels for 0% -> 0%
where the time goes in v1:
time: 1020 us; the launch traced here: 1010 us
  local copies, waits for them, and re-layouts  292 us (29%)
  waiting for transfers between devices  239 us (23%)
  blocking collectives  226 us (22%)
  other arithmetic  119 us (12%)
  matrix products  93.8 us (9%)
  starting transfers between devices  27.7 us (3%)
  between operations  15 us (1%)
    all_to_all x1, blocking collectives, check_ports(): lax.all_to_all(jnp.stack([local_block for _ in range(lax.axis_size(group_...  136 us
    all_to_all x1, waiting for transfers between devices, check_ports(): lax.all_to_all(jnp.stack([local_block for _ in range(lax.axis_size(group_...  128 us
    unnamed x75, local copies, waits for them, and re-layouts  123 us
    all_to_all x2, other arithmetic, check_ports(): lax.all_to_all(jnp.stack([local_block for _ in range(lax.axis_size(group_...  108 us
    all_gather x2, waiting for transfers between devices, synthesize(): portion = lax.all_gather(spectrum, 'gx', axis=3, tiled=True)  95.4 us
    psum x1, blocking collectives, local(): lax.psum((local_weight, local_bias), ('gx', 'gy'))  77.1 us
    reshape x2, local copies, waits for them, and re-layouts, check_ports(): jnp.concatenate(lax.all_to_all(jnp.stack([local_block for _ in range(lax....  26.4 us
    squeeze x4, local copies, waits for them, and re-layouts, synthesize(): blocks[1]  24.3 us
  transfers between devices with their start and end apart: 6, of which 4 were waited for; matrix products, arithmetic and copies ran while one was open for 3% of the time, Pallas kernels for 0%

profile of v1, /device:TPU:1, one launch (start us, length us, event | category | flops | bytes accessed | tf_op | source)
XLA Modules:
  0.0 1012.6 jit_solution(10077876600174489311)
XLA Ops:
  19.7 7.1 all-to-all-start
  26.9 9.1 all-to-all-done
  43.6 6.3 copy.277
  54.5 7.5 stack.58
  62.0 20.2 %reshape.245 = f32[32,1,46080]{2,1,0:T(1,128)} reshape(f32[32,3,2,20,8,48]{5,4,3,2,1,0:T(8,128)} %stack.58) | data formatting | bytes 11796480
  82.2 10.6 %all-to-all-start.1 = ((f32[32,1,46080]{2,1,0:T(1,128)}), f32[32,1,46080]{2,1,0:T(1,128)}, u32[]{:S(2)}, u32[]{:S(2)}) async-start(f32[32,1,46080]{2,1,0:T(1,128)} %reshape.245), calls=%async_computation.1 | async-start | bytes 11796480 | tf_op jit(solution)/shard_map/all_to_all | solution.py:17
  94.0 127.7 %all-to-all-done.1 = f32[32,1,46080]{2,1,0:T(1,128)} async-done(((f32[32,1,46080]{2,1,0:T(1,128)}), f32[32,1,46080]{2,1,0:T(1,128)}, u32[]{:S(2)}, u32[]{:S(2)}) %all-to-all-start.1) | async-done | bytes 5898272 | tf_op jit(solution)/shard_map/all_to_all | solution.py:17
  221.7 54.2 %reduce.18 = f32[32,46080]{1,0:T(8,128)} reduce(f32[32,1,46080]{2,1,0:T(1,128)} %all-to-all-done.1, f32[]{:T(128)} %broadcast.402), dimensions={1}, to_apply=%all_to_all.53.reduce_sub_computation | reduce | bytes 11796484 | tf_op jit(solution)/shard_map/all_to_all | solution.py:17
  275.9 11.2 %reshape.246 = f32[32,3,2,20,8,48]{5,4,3,2,1,0:T(8,128)} reshape(f32[32,46080]{1,0:T(8,128)} %reduce.18) | data formatting | bytes 11796480
  287.1 13.2 %copy_bitcast_fusion.1 = f32[3,2,20,256,48]{4,3,2,1,0:T(8,128)} fusion(f32[32,3,2,20,8,48]{5,4,3,2,1,0:T(8,128)} %reshape.246), kind=kLoop, calls=%fused_computation.1 | loop fusion | bytes 11796480 | tf_op jit(solution)/shard_map/reshape | solution.py:16
  300.3 7.2 fusion
  307.5 7.1 fusion.1
  324.5 95.4 %all-gather.3.cloned.1.call-done = f32[2,20,3,2304]{1,0,2,3:T(2,128)} async-done(((f32[2,20,3,72]{1,0,2,3:T(2,128)}), f32[2,20,3,2304]{1,0,2,3:T(2,128)}) %all-gather.3.cloned.1.call-update) | async-done | bytes 1105936 | tf_op jit(solution)/shard_map/all_gather | solution.py:116
  420.0 10.0 fusion.244
  430.0 11.2 %copy.401 = f32[1,20,3,2304]{3,2,1,0:T(4,128)} copy(f32[1,20,3,2304]{1,0,2,3:T(1,128)} %get-tuple-element.59) | data formatting | bytes 1105920 | tf_op jit(solution)/shard_map/squeeze | solution.py:122
  446.4 11.2 %copy.402 = f32[1,20,3,2304]{3,2,1,0:T(4,128)} copy(f32[1,20,3,2304]{1,0,2,3:T(1,128)} %get-tuple-element.58) | data formatting | bytes 1105920 | tf_op jit(solution)/shard_map/squeeze | solution.py:123
  481.0 6.3 all-to-all-done.2
  506.5 10.1 fusion.241
  529.6 12.3 %all_to_all.70 = f32[8,1,15360]{2,1,0:T(1,128)S(1)} all-to-all(f32[8,1,15360]{2,1,0:T(1,128)S(1)} %reshape.249), channel_id=1, replica_groups=mesh['gx'=32,'gy'=8] {'gy'}, dimensions={0} | all-to-all | bytes 983040 | tf_op jit(solution)/shard_map/all_to_all | solution.py:108
  549.1 6.3 copy.301
  560.0 7.5 stack.70
  567.4 20.2 %reshape.251 = f32[32,1,46080]{2,1,0:T(1,128)} reshape(f32[32,3,2,20,8,48]{5,4,3,2,1,0:T(8,128)} %stack.70) | data formatting | bytes 11796480
  587.6 136.5 %all_to_all.71 = f32[32,1,46080]{2,1,0:T(1,128)} all-to-all(f32[32,1,46080]{2,1,0:T(1,128)} %reshape.251), channel_id=1, replica_groups=mesh['gx'=32,'gy'=8] {'gx'}, dimensions={0} | all-to-all | bytes 11796480 | tf_op jit(solution)/shard_map/all_to_all | solution.py:17
  724.1 54.2 %reduce.21 = f32[32,46080]{1,0:T(8,128)} reduce(f32[32,1,46080]{2,1,0:T(1,128)} %all_to_all.71, f32[]{:T(128)} %broadcast.402), dimensions={1}, to_apply=%all_to_all.60.reduce_sub_computation | reduce | bytes 11796484 | tf_op jit(solution)/shard_map/all_to_all | solution.py:17
  778.3 11.4 %reshape.252 = f32[32,3,2,20,8,48]{5,4,3,2,1,0:T(8,128)} reshape(f32[32,46080]{1,0:T(8,128)} %reduce.21) | data formatting | bytes 11796480
  789.7 13.2 %copy_bitcast_fusion = f32[3,2,20,256,48]{4,3,2,1,0:T(8,128)} fusion(f32[32,3,2,20,8,48]{5,4,3,2,1,0:T(8,128)} %reshape.252), kind=kLoop, calls=%fused_computation | loop fusion | bytes 11796480 | tf_op jit(solution)/shard_map/reshape | solution.py:16
  802.9 7.2 fusion.4
  810.1 7.1 fusion.5
  837.7 77.1 %all-reduce = (f32[20,20]{0,1:T(8,128)S(1)}, f32[20]{0:T(128)S(1)}) all-reduce(f32[20,20]{0,1:T(8,128)S(1)} %fusion.36, f32[20]{0:T(128)S(1)} %copy-done.24), channel_id=1, replica_groups=mesh['gx'=32,'gy'=8] {'gx','gy'}, use_global_device_ids=true, to_apply=%region_0.1 | all-reduce | flops 420 | bytes 3360 | tf_op jit(solution)/shard_map/psum | solution.py:175
  919.8 10.0 fusion.243
  929.8 9.8 copy.405
  943.8 9.8 copy.406
  (169 shorter events, 189.6 us)
Async XLA Ops:
  7.2 1.3 copy-start
  8.5 508.1 %copy-start.10 = (f32[256,48,1,1]{0,1,2,3:T(8,128)}, f32[256,48,1,1]{0,1,2,3:T(8,128)S(1)}, u32[]{:S(2)}) copy-start(f32[256,48,1,1]{0,1,2,3:T(8,128)S(1)} %reshape.214) | copy-start | bytes 147460
  19.7 16.2 %all-to-all-start = ((f32[8,1,15360]{2,1,0:T(1,128)}), f32[8,1,15360]{2,1,0:T(1,128)S(1)}, u32[]{:S(2)}, u32[]{:S(2)}) async-start(f32[8,1,15360]{2,1,0:T(1,128)} %reshape.243), calls=%async_computation | async-start | bytes 983040 | tf_op jit(solution)/shard_map/all_to_all | solution.py:108
  82.2 10.9 %copy-start.9 = (bf16[2,20,20,3,72]{4,0,3,2,1:T(2,128)(2,1)S(1)}, bf16[2,20,20,3,72]{4,0,3,2,1:T(2,128)(2,1)}, u32[]{:S(2)}) copy-start(bf16[2,20,20,3,72]{4,0,3,2,1:T(2,128)(2,1)} %param.7) | copy-start | bytes 1036804
  82.2 139.5 %all-to-all-start.1 = ((f32[32,1,46080]{2,1,0:T(1,128)}), f32[32,1,46080]{2,1,0:T(1,128)}, u32[]{:S(2)}, u32[]{:S(2)}) async-start(f32[32,1,46080]{2,1,0:T(1,128)} %reshape.245), calls=%async_computation.1 | async-start | bytes 11796480 | tf_op jit(solution)/shard_map/all_to_all | solution.py:17
  92.8 327.2 %all-gather.3.cloned.1.call-start = ((), (), s32[]{:S(2)}) async-start(), calls=%async_computation.6 | async-start | bytes 7299072 | tf_op jit(solution)/shard_map/all_gather | solution.py:116
  93.0 225.8 %copy-start.18 = (s32[3]{0:T(128)}, s32[3]{0:T(128)S(1)}, u32[]{:S(2)}) copy-start(s32[3]{0:T(128)S(1)} %compare_select_fusion) | copy-start | bytes 40
  93.1 230.5 %copy-start.22 = (f32[3]{0:T(128)}, f32[3]{0:T(128)S(1)}, u32[]{:S(2)}) copy-start(f32[3]{0:T(128)S(1)} %fusion.144) | copy-start | bytes 40
  94.0 229.2 %copy-start.5 = (bf16[1,20,20,3,72]{4,0,3,2,1:T(2,128)(2,1)}, bf16[1,20,20,3,72]{4,0,3,2,1:T(2,128)(2,1)S(1)}, u32[]{:S(2)}) copy-start(bf16[1,20,20,3,72]{4,0,3,2,1:T(2,128)(2,1)S(1)} %get-tuple-element.70) | copy-start | bytes 518404
  300.3 14.3 %copy-start.2 = (f32[3,2,20,256,48]{4,3,2,1,0:T(8,128)S(1)}, f32[3,2,20,256,48]{4,3,2,1,0:T(8,128)}, u32[]{:S(2)}) copy-start(f32[3,2,20,256,48]{4,3,2,1,0:T(8,128)} %copy_bitcast_fusion.1) | copy-start | bytes 17694724
  323.1 106.9 %copy-start.12 = (f32[3,72,20]{1,0,2:T(4,128)}, f32[3,72,20]{1,0,2:T(4,128)S(1)}, u32[]{:S(2)}) copy-start(f32[3,72,20]{1,0,2:T(4,128)S(1)} %copy.416) | copy-start | bytes 51844
  323.1 106.8 %copy-start.14 = (f32[3,72,20]{1,0,2:T(4,128)}, f32[3,72,20]{1,0,2:T(4,128)S(1)}, u32[]{:S(2)}) copy-start(f32[3,72,20]{1,0,2:T(4,128)S(1)} %copy.415) | copy-start | bytes 51844
  324.5 137.1 %copy-start.16 = (s32[8]{0:T(128)}, s32[8]{0:T(128)S(1)}, u32[]{:S(2)}) copy-start(s32[8]{0:T(128)S(1)} %iota_add_fusion.1) | copy-start | bytes 100
  467.3 10.9 %copy-start.20 = (bf16[20,20]{1,0:T(8,128)(2,1)S(1)}, bf16[20,20]{1,0:T(8,128)(2,1)}, u32[]{:S(2)}) copy-start(bf16[20,20]{1,0:T(8,128)(2,1)} %param.8) | copy-start | bytes 2404
  472.8 14.5 %all-to-all-start.2 = ((f32[8,1,15360]{2,1,0:T(1,128)}), f32[8,1,15360]{2,1,0:T(1,128)S(1)}, u32[]{:S(2)}, u32[]{:S(2)}) async-start(f32[8,1,15360]{2,1,0:T(1,128)} %reshape.247), calls=%async_computation.2 | async-start | bytes 983040 | tf_op jit(solution)/shard_map/all_to_all | solution.py:129
  478.2 441.6 %all-gather.5.cloned.1.call-start = ((), (), s32[]{:S(2)}) async-start(), calls=%async_computation.7 | async-start | bytes 7299072 | tf_op jit(solution)/shard_map/all_gather | solution.py:116
  500.7 5.8 copy-start.25
  516.6 1.6 copy-start.3
  789.7 13.2 %copy-start.19 = (s32[3]{0:T(128)S(1)}, s32[3]{0:T(128)}, u32[]{:S(2)}) copy-start(s32[3]{0:T(128)} %copy-done.18) | copy-start | bytes 40
  802.9 14.3 %copy-start.1 = (f32[3,2,20,256,48]{4,3,2,1,0:T(8,128)S(1)}, f32[3,2,20,256,48]{4,3,2,1,0:T(8,128)}, u32[]{:S(2)}) copy-start(f32[3,2,20,256,48]{4,3,2,1,0:T(8,128)} %copy_bitcast_fusion) | copy-start | bytes 17694724
  821.2 4.3 copy-start.23
  821.2 4.3 copy-start.6
  821.2 4.4 copy-start.13
  821.2 4.4 copy-start.15
  831.5 3.5 copy-start.4
  835.0 2.7 copy-start.24
  835.0 79.8 %copy-start.21 = (bf16[20,20]{1,0:T(8,128)(2,1)S(1)}, bf16[20,20]{1,0:T(8,128)(2,1)}, u32[]{:S(2)}) copy-start(bf16[20,20]{1,0:T(8,128)(2,1)} %param.8) | copy-start | bytes 2404
  929.8 10.9 %copy-start.17 = (s32[8]{0:T(128)S(1)}, s32[8]{0:T(128)}, u32[]{:S(2)}) copy-start(s32[8]{0:T(128)} %copy-done.16) | copy-start | bytes 100
  967.7 15.2 %all-to-all-start.5 = ((f32[8,1,15360]{2,1,0:T(1,128)}), f32[8,1,15360]{2,1,0:T(1,128)S(1)}, u32[]{:S(2)}, u32[]{:S(2)}) async-start(f32[8,1,15360]{2,1,0:T(1,128)} %reshape.253), calls=%async_computation.5 | async-start | bytes 983040 | tf_op jit(solution)/shard_map/all_to_all | solution.py:129
  978.4 2.4 copy-start.7
  978.4 2.3 copy-start.8
  995.8 4.8 copy-start.11
Sparse Core Ops, SparseCore 0:
  324.6 95.3 all-gather.2
  828.5 88.4 all-gather.4
